TPU v7x, 256 devices: a whole 4x4x8 slice. The times are simulated.
256 devices in a mesh: tm: 8 (over x_hi, y), azim: 32 (over z, x_lo, core).
Axes of the slice: x: 4 (x_hi: 2, x_lo: 2; x = x_hi * 2 + x_lo), y: 4, z: 8, core: 2. Of those that a mesh axis runs over, the one named last changes fastest.
Arguments:
- rotor_coeffs: float32 [64, 2, 32, 16384], P('tm', None, 'azim'), may hold values from -1.5 to 1.5
- mortar_weights: float32 [64, 2, 32, 16384], P('tm', None, 'azim'), may hold values from 0.2 to 1
- block_shifts: int32 [64], P('tm'), may hold values from 0 to 31
- stencil_offsets: int32 [64, 2], P('tm'), may hold values from -1 to 1
- reluctivity: float32 [32, 16384], P('azim'), may hold values from 0.5 to 2
- source: float32 [64, 2, 32, 16384], P('tm', None, 'azim'), may hold values from -3 to 3
Outputs:
- residual: float32 [64, 2, 32, 16384], P('tm', None, 'azim')
All inputs are finite; a program needn't handle non-finite values.
Results may differ from a plain program's by a relative error of at most 0.0001.
Values sent between devices are 32-bit elements; how exact they have to be, the bound alone decides.
A program may use at most 128 MiB of HBM per device.

v0:
```python
import jax
import jax.numpy as jnp
from jax import lax
from jax.sharding import PartitionSpec as P

KC = 64
NT = 64
LANES = 128


def shifted(value, axis, steps):
    count = lax.axis_size(axis)
    pairs = [(source, (source + steps) % count) for source in range(count)]
    return lax.ppermute(value, axis, pairs)


def harmonic_basis(sample_rows, coefficient_count):
    column = jnp.arange(coefficient_count, dtype=jnp.int32)
    harmonic_order = 2 * (column // 2) + 1
    phase_index = harmonic_order[None, :] * (2 * sample_rows[:, None] + 1) % (4 * NT)
    phase_angle = phase_index.astype(jnp.float32) * (jnp.pi / (2 * NT))
    return jnp.where(column[None, :] % 2 == 0, jnp.cos(phase_angle), jnp.sin(phase_angle))


def per_sample(flags, value):
    return flags.reshape((-1,) + (1,) * (value.ndim - 1))


def body(rotor_coeffs, mortar_weights, block_shifts, stencil_offsets, reluctivity, source):
    local_c, comp, _, nodes = rotor_coeffs.shape
    local_j, sten = mortar_weights.shape[:2]
    rows = nodes // LANES
    parts = lax.axis_size("tm")
    chunk = rows // parts
    coeffs = lax.all_to_all(
        rotor_coeffs.reshape(local_c, comp, rows, LANES),
        "tm",
        split_axis=2,
        concat_axis=0,
        tiled=True,
    )
    weights = lax.all_to_all(
        mortar_weights.reshape(local_j, sten, rows, LANES),
        "tm",
        split_axis=2,
        concat_axis=0,
        tiled=True,
    )
    shifts = lax.all_gather(block_shifts, "tm", tiled=True)
    offsets = lax.all_gather(stencil_offsets, "tm", tiled=True)
    gain = lax.dynamic_slice_in_dim(
        reluctivity.reshape(rows, LANES), lax.axis_index("tm") * chunk, chunk, axis=0
    )
    table = harmonic_basis(jnp.arange(NT, dtype=jnp.int32), KC)
    samples = jnp.einsum("jc,capk->japk", table, coeffs, precision=lax.Precision.HIGHEST)
    turned = samples
    for bit_level in range((lax.axis_size("azim") - 1).bit_length()):
        moved = shifted(turned, "azim", 1 << bit_level)
        chosen = shifts >> bit_level & 1 == 1
        turned = jnp.where(per_sample(chosen, turned), moved, turned)
    from_left = shifted(turned, "azim", 1)
    from_right = shifted(turned, "azim", -1)
    airgap_field = jnp.zeros_like(samples)
    for stencil_entry in range(sten):
        offset = offsets[:, stencil_entry]
        neighbour = jnp.where(
            per_sample(offset == 0, turned),
            turned,
            jnp.where(per_sample(offset > 0, turned), from_right, from_left),
        )
        airgap_field = airgap_field + weights[:, stencil_entry][:, None] * neighbour
    square = jnp.sum(airgap_field * airgap_field, axis=1, keepdims=True)
    field_flux = gain[None, None] * (1.0 + square / (1.0 + square)) * airgap_field
    summed = jnp.einsum(
        "jc,japk->capk", table * (2.0 / NT), field_flux, precision=lax.Precision.HIGHEST
    )
    residual = lax.all_to_all(summed, "tm", split_axis=0, concat_axis=2, tiled=True)
    return residual.reshape(source.shape) - source


def solution(mesh):
    in_specs = (
        P("tm", None, "azim", None),
        P("tm", None, "azim", None),
        P("tm"),
        P("tm", None),
        P("azim", None),
        P("tm", None, "azim", None),
    )
    out_specs = P("tm", None, "azim", None)
    return jax.shard_map(body, mesh=mesh, in_specs=in_specs, out_specs=out_specs, check_vma=False)
```

profile of v0, /device:TPU:97, one launch (start us, length us, event | category | flops | bytes accessed | tf_op | source)
XLA Modules:
  0.0 303.6 jit_solution(7695853863553865588)
XLA Ops:
  0.0 0.0 copy-start
  0.0 3.0 copy.28
  3.0 6.7 %all-to-all-start.1 = ((f32[8,2,128,128]{3,1,0,2:T(2,128)}), f32[8,2,128,128]{3,1,0,2:T(2,128)S(1)}, u32[]{:S(2)}, u32[]{:S(2)}) async-start(f32[8,2,128,128]{3,1,0,2:T(2,128)} %copy.28), calls=%async_computation.1 | async-start | bytes 2097152 | tf_op jit(solution)/shard_map/all_to_all | solution.py:35
  9.7 14.2 %all-to-all-done.1 = f32[8,2,128,128]{3,1,0,2:T(2,128)S(1)} async-done(((f32[8,2,128,128]{3,1,0,2:T(2,128)}), f32[8,2,128,128]{3,1,0,2:T(2,128)S(1)}, u32[]{:S(2)}, u32[]{:S(2)}) %all-to-all-start.1) | async-done | bytes 1048608 | tf_op jit(solution)/shard_map/all_to_all | solution.py:35
  23.9 0.3 copy.29
  24.2 1.8 fusion
  26.0 2.9 collective-permute-start
  28.9 0.0 copy-start.6
  28.9 0.7 copy-done.6
  29.6 0.6 dynamic-slice
  30.8 0.0 copy-start.5
  30.8 0.6 copy-done.5
  31.4 0.2 dynamic-update-slice
  31.6 11.8 %all-reduce = s32[64]{0:T(128)S(1)} all-reduce(s32[64]{0:T(128)S(1)} %dynamic-update-slice), channel_id=1, replica_groups=mesh['tm'=8,'azim'=32] {'tm'}, use_global_device_ids=true, to_apply=%add | all-reduce | flops 64 | bytes 512
  43.4 0.0 collective-permute-done
  43.4 0.2 broadcast_select_fusion
  43.7 1.0 collective-permute-start.1
  44.7 24.2 %collective-permute-done.1 = f32[64,2,16,128]{3,0,2,1:T(8,128)S(1)} collective-permute-done((f32[64,2,16,128]{3,0,2,1:T(8,128)S(1)}, f32[64,2,16,128]{3,0,2,1:T(8,128)S(1)}, u32[]{:S(2)}, u32[]{:S(2)}) %collective-permute-start.1) | collective-permute-done | bytes 1048608 | tf_op jit(solution)/shard_map/ppermute | solution.py:14
  68.9 0.2 broadcast_select_fusion.1
  69.2 3.4 %collective-permute-start.2 = (f32[64,2,16,128]{3,0,2,1:T(8,128)S(1)}, f32[64,2,16,128]{3,0,2,1:T(8,128)S(1)}, u32[]{:S(2)}, u32[]{:S(2)}) collective-permute-start(f32[64,2,16,128]{3,0,2,1:T(8,128)S(1)} %broadcast_select_fusion.1), channel_id=1, source_target_pairs={{0,4},{1,5},{2,6},{3,7},{4,8},{5,9},{6,10},{7,11},{8,12},{9,13},{1... | collective-permute-start | bytes 3145736 | tf_op jit(solution)/shard_map/ppermute | solution.py:14
  72.6 20.1 %collective-permute-done.2 = f32[64,2,16,128]{3,0,2,1:T(8,128)S(1)} collective-permute-done((f32[64,2,16,128]{3,0,2,1:T(8,128)S(1)}, f32[64,2,16,128]{3,0,2,1:T(8,128)S(1)}, u32[]{:S(2)}, u32[]{:S(2)}) %collective-permute-start.2) | collective-permute-done | bytes 1048608 | tf_op jit(solution)/shard_map/ppermute | solution.py:14
  92.7 0.2 broadcast_select_fusion.2
  93.0 2.8 collective-permute-start.3
  95.7 28.5 %collective-permute-done.3 = f32[64,2,16,128]{3,0,2,1:T(8,128)S(1)} collective-permute-done((f32[64,2,16,128]{3,0,2,1:T(8,128)S(1)}, f32[64,2,16,128]{3,0,2,1:T(8,128)S(1)}, u32[]{:S(2)}, u32[]{:S(2)}) %collective-permute-start.3) | collective-permute-done | bytes 1048608 | tf_op jit(solution)/shard_map/ppermute | solution.py:14
  124.2 0.0 copy-start.2
  124.2 0.2 broadcast_select_fusion.3
  124.5 5.7 %collective-permute-start.4 = (f32[64,2,16,128]{3,0,2,1:T(8,128)S(1)}, f32[64,2,16,128]{3,0,2,1:T(8,128)S(1)}, u32[]{:S(2)}, u32[]{:S(2)}) collective-permute-start(f32[64,2,16,128]{3,0,2,1:T(8,128)S(1)} %broadcast_select_fusion.3), channel_id=1, source_target_pairs={{0,16},{1,17},{2,18},{3,19},{4,20},{5,21},{6,22},{7,23},{8,24},{9,... | collective-permute-start | bytes 3145736 | tf_op jit(solution)/shard_map/ppermute | solution.py:14
  130.2 0.0 copy-done.2
  130.2 1.8 copy.24
  132.0 8.7 %all-to-all-start = ((f32[8,2,128,128]{3,1,0,2:T(2,128)}), f32[8,2,128,128]{3,1,0,2:T(2,128)S(1)}, u32[]{:S(2)}, u32[]{:S(2)}) async-start(f32[8,2,128,128]{3,1,0,2:T(2,128)} %copy.24), calls=%async_computation | async-start | bytes 2097152 | tf_op jit(solution)/shard_map/all_to_all | solution.py:42
  140.7 33.7 %collective-permute-done.4 = f32[64,2,16,128]{3,0,2,1:T(8,128)S(1)} collective-permute-done((f32[64,2,16,128]{3,0,2,1:T(8,128)S(1)}, f32[64,2,16,128]{3,0,2,1:T(8,128)S(1)}, u32[]{:S(2)}, u32[]{:S(2)}) %collective-permute-start.4) | collective-permute-done | bytes 1048608 | tf_op jit(solution)/shard_map/ppermute | solution.py:14
  174.4 0.0 copy-start.3
  174.4 1.0 copy-done.3
  175.4 1.4 broadcast_select_fusion.4
  176.8 20.0 %collective-permute-start.6 = (f32[64,2,16,128]{3,0,2,1:T(8,128)S(1)}, f32[64,2,16,128]{3,0,2,1:T(8,128)S(1)}, u32[]{:S(2)}, u32[]{:S(2)}) collective-permute-start(f32[64,2,16,128]{3,0,2,1:T(8,128)S(1)} %broadcast_select_fusion.4), channel_id=1, source_target_pairs={{0,1},{1,2},{2,3},{3,4},{4,5},{5,6},{6,7},{7,8},{8,9},{9,10},{10,1... | collective-permute-start | bytes 3145736 | tf_op jit(solution)/shard_map/ppermute | solution.py:14
  196.8 0.0 collective-permute-start.5
  196.8 0.0 copy-start.4
  196.8 0.7 copy-done.4
  197.4 52.3 %all-gather = s32[8,8,2]{1,2,0:T(2,128)S(1)} all-gather(s32[1,8,2]{1,2,0:T(2,128)S(1)} %bitcast.51), channel_id=1, replica_groups=mesh['tm'=8,'azim'=32] {'tm'}, dimensions={0}, use_global_device_ids=true | all-gather | bytes 576 | tf_op jit(solution)/shard_map/all_gather | solution.py:50
  249.8 0.1 reshape.115
  249.9 0.0 copy-done
  249.9 0.0 all-to-all-done
  249.9 0.1 copy.46
  250.0 0.1 slice_bitcast_fusion.1
  250.1 0.0 collective-permute-done.6
  250.1 0.0 collective-permute-done.5
  250.1 1.9 multiply_reduce_fusion
  252.0 0.1 fusion.6
  252.1 1.2 fusion.3
  253.3 0.6 copy.32
  254.0 46.4 %all_to_all.51 = f32[64,2,16,128]{3,2,1,0:T(8,128)S(1)} all-to-all(f32[64,2,16,128]{3,2,1,0:T(8,128)S(1)} %copy.32), channel_id=1, replica_groups=mesh['tm'=8,'azim'=32] {'tm'}, dimensions={0} | all-to-all | bytes 2097152 | tf_op jit(solution)/shard_map/all_to_all | solution.py:77
  300.3 0.0 copy-start.1
  300.3 0.1 copy.33
  300.4 1.1 copy-done.1
  301.5 2.1 sub.12
  (7 shorter events, 0.0 us)
Async XLA Ops:
  0.0 249.9 %copy-start = (f32[1,16384]{1,0:T(1,128)S(1)}, f32[1,16384]{1,0:T(1,128)}, u32[]{:S(2)}) copy-start(f32[1,16384]{1,0:T(1,128)} %param.10) | copy-start | bytes 196612
  3.0 20.8 %all-to-all-start.1 = ((f32[8,2,128,128]{3,1,0,2:T(2,128)}), f32[8,2,128,128]{3,1,0,2:T(2,128)S(1)}, u32[]{:S(2)}, u32[]{:S(2)}) async-start(f32[8,2,128,128]{3,1,0,2:T(2,128)} %copy.28), calls=%async_computation.1 | async-start | bytes 2097152 | tf_op jit(solution)/shard_map/all_to_all | solution.py:35
  26.0 17.4 %collective-permute-start = (f32[64,2,16,128]{3,0,2,1:T(8,128)S(1)}, f32[64,2,16,128]{3,0,2,1:T(8,128)S(1)}, u32[]{:S(2)}, u32[]{:S(2)}) collective-permute-start(f32[64,2,16,128]{3,0,2,1:T(8,128)S(1)} %fusion), channel_id=1, source_target_pairs={{0,1},{1,2},{2,3},{3,4},{4,5},{5,6},{6,7},{7,8},{8,9},{9,10},{10,1... | collective-permute-start | bytes 3145736 | tf_op jit(solution)/shard_map/ppermute | solution.py:14
  28.9 0.7 copy-start.6
  30.8 0.7 copy-start.5
  43.7 25.3 %collective-permute-start.1 = (f32[64,2,16,128]{3,0,2,1:T(8,128)S(1)}, f32[64,2,16,128]{3,0,2,1:T(8,128)S(1)}, u32[]{:S(2)}, u32[]{:S(2)}) collective-permute-start(f32[64,2,16,128]{3,0,2,1:T(8,128)S(1)} %broadcast_select_fusion), channel_id=1, source_target_pairs={{0,2},{1,3},{2,4},{3,5},{4,6},{5,7},{6,8},{7,9},{8,10},{9,11},{10,... | collective-permute-start | bytes 3145736 | tf_op jit(solution)/shard_map/ppermute | solution.py:14
  69.2 23.6 %collective-permute-start.2 = (f32[64,2,16,128]{3,0,2,1:T(8,128)S(1)}, f32[64,2,16,128]{3,0,2,1:T(8,128)S(1)}, u32[]{:S(2)}, u32[]{:S(2)}) collective-permute-start(f32[64,2,16,128]{3,0,2,1:T(8,128)S(1)} %broadcast_select_fusion.1), channel_id=1, source_target_pairs={{0,4},{1,5},{2,6},{3,7},{4,8},{5,9},{6,10},{7,11},{8,12},{9,13},{1... | collective-permute-start | bytes 3145736 | tf_op jit(solution)/shard_map/ppermute | solution.py:14
  93.0 31.3 %collective-permute-start.3 = (f32[64,2,16,128]{3,0,2,1:T(8,128)S(1)}, f32[64,2,16,128]{3,0,2,1:T(8,128)S(1)}, u32[]{:S(2)}, u32[]{:S(2)}) collective-permute-start(f32[64,2,16,128]{3,0,2,1:T(8,128)S(1)} %broadcast_select_fusion.2), channel_id=1, source_target_pairs={{0,8},{1,9},{2,10},{3,11},{4,12},{5,13},{6,14},{7,15},{8,16},{9,17... | collective-permute-start | bytes 3145736 | tf_op jit(solution)/shard_map/ppermute | solution.py:14
  124.2 5.9 %copy-start.2 = (f32[8,2,1,16384]{3,2,1,0:T(1,128)S(1)}, f32[8,2,1,16384]{3,2,1,0:T(1,128)}, u32[]{:S(2)}) copy-start(f32[8,2,1,16384]{3,2,1,0:T(1,128)} %param.7) | copy-start | bytes 3145732
  124.5 49.9 %collective-permute-start.4 = (f32[64,2,16,128]{3,0,2,1:T(8,128)S(1)}, f32[64,2,16,128]{3,0,2,1:T(8,128)S(1)}, u32[]{:S(2)}, u32[]{:S(2)}) collective-permute-start(f32[64,2,16,128]{3,0,2,1:T(8,128)S(1)} %broadcast_select_fusion.3), channel_id=1, source_target_pairs={{0,16},{1,17},{2,18},{3,19},{4,20},{5,21},{6,22},{7,23},{8,24},{9,... | collective-permute-start | bytes 3145736 | tf_op jit(solution)/shard_map/ppermute | solution.py:14
  132.0 117.9 %all-to-all-start = ((f32[8,2,128,128]{3,1,0,2:T(2,128)}), f32[8,2,128,128]{3,1,0,2:T(2,128)S(1)}, u32[]{:S(2)}, u32[]{:S(2)}) async-start(f32[8,2,128,128]{3,1,0,2:T(2,128)} %copy.24), calls=%async_computation | async-start | bytes 2097152 | tf_op jit(solution)/shard_map/all_to_all | solution.py:42
  174.4 1.0 copy-start.3
  176.8 73.3 %collective-permute-start.6 = (f32[64,2,16,128]{3,0,2,1:T(8,128)S(1)}, f32[64,2,16,128]{3,0,2,1:T(8,128)S(1)}, u32[]{:S(2)}, u32[]{:S(2)}) collective-permute-start(f32[64,2,16,128]{3,0,2,1:T(8,128)S(1)} %broadcast_select_fusion.4), channel_id=1, source_target_pairs={{0,1},{1,2},{2,3},{3,4},{4,5},{5,6},{6,7},{7,8},{8,9},{9,10},{10,1... | collective-permute-start | bytes 3145736 | tf_op jit(solution)/shard_map/ppermute | solution.py:14
  196.8 53.4 %collective-permute-start.5 = (f32[64,2,16,128]{3,0,2,1:T(8,128)S(1)}, f32[64,2,16,128]{3,0,2,1:T(8,128)}, u32[]{:S(2)}, u32[]{:S(2)}) collective-permute-start(f32[64,2,16,128]{3,0,2,1:T(8,128)S(1)} %broadcast_select_fusion.4), channel_id=1, source_target_pairs={{0,31},{1,0},{2,1},{3,2},{4,3},{5,4},{6,5},{7,6},{8,7},{9,8},{10,9... | collective-permute-start | bytes 3145736 | tf_op jit(solution)/shard_map/ppermute | solution.py:14
  196.8 0.7 copy-start.4
  300.3 1.2 copy-start.1
where the time goes:
time: 304 us
  waiting for transfers between devices  121 us (40%)
  blocking collectives  110 us (36%)
  starting transfers between devices  51.1 us (17%)
  local copies, waits for them, and re-layouts  11 us (4%)
  other arithmetic  6.42 us (2%)
    ppermute x7, waiting for transfers between devices, shifted(): return lax.ppermute(value, axis, pairs)  107 us
    all_gather x1, blocking collectives, body(): offsets = lax.all_gather(stencil_offsets, 'tm', tiled=True)  52.3 us
    all_to_all x1, blocking collectives, body(): lax.all_to_all(summed, 'tm', split_axis=0, concat_axis=2, tiled=True)  46.4 us
    ppermute x7, starting transfers between devices, shifted(): return lax.ppermute(value, axis, pairs)  35.7 us
    all_to_all x1, waiting for transfers between devices, body(): lax.all_to_all(rotor_coeffs.reshape(local_c, comp, rows, LANES), 'tm', sp...  14.2 us
    unnamed x1, blocking collectives  11.8 us
    all_to_all x1, starting transfers between devices, body(): lax.all_to_all(mortar_weights.reshape(local_j, sten, rows, LANES), 'tm',...  8.69 us
    all_to_all x1, starting transfers between devices, body(): lax.all_to_all(rotor_coeffs.reshape(local_c, comp, rows, LANES), 'tm', sp...  6.65 us
  transfers between devices with their start and end apart: 9, of which 5 were waited for; matrix products, arithmetic and copies ran while one was open for 1% of the time, Pallas kernels for 0%

commit v1 on v0

--- a/solution.py
+++ b/solution.py
@@ -47,7 +47,9 @@
         tiled=True,
     )
     shifts = lax.all_gather(block_shifts, "tm", tiled=True)
-    offsets = lax.all_gather(stencil_offsets, "tm", tiled=True)
+    offsets = jnp.concatenate(
+        lax.all_to_all(jnp.stack([stencil_offsets] * lax.axis_size("tm")), "tm", 0, 0), axis=0
+    )
     gain = lax.dynamic_slice_in_dim(
         reluctivity.reshape(rows, LANES), lax.axis_index("tm") * chunk, chunk, axis=0
     )

time: 304 us -> 291 us (0.957)
  blocking collectives: 110 us -> 65.3 us
  waiting for transfers between devices: 121 us -> 139 us
  starting transfers between devices: 51.1 us -> 64.1 us
    all_gather x1 -> x0, blocking collectives: 52.3 us -> none  [body(): offsets = lax.all_gather(stencil_offsets, 'tm', tiled=True)]
    ppermute x7, waiting for transfers between devices: 107 us -> 121 us  [shifted(): return lax.ppermute(value, axis, pairs)]
    ppermute x7, starting transfers between devices: 35.7 us -> 45.2 us  [shifted(): return lax.ppermute(value, axis, pairs)]
    all_to_all x0 -> x1, starting transfers between devices: none -> 8.69 us  [body(): lax.all_to_all(jnp.stack([stencil_offsets] * lax.axis_size('tm')), 'tm',...]
    all_to_all x1, blocking collectives: 46.4 us -> 53.6 us  [body(): lax.all_to_all(summed, 'tm', split_axis=0, concat_axis=2, tiled=True)]
    all_to_all x1, starting transfers between devices: 8.69 us -> 3.56 us  [body(): lax.all_to_all(mortar_weights.reshape(local_j, sten, rows, LANES), 'tm',...]
    all_to_all x0 -> x1, waiting for transfers between devices: none -> 4.76 us  [body(): lax.all_to_all(jnp.stack([stencil_offsets] * lax.axis_size('tm')), 'tm',...]
  transfers between devices with their start and end apart: 9 -> 10, of which waited for: 5 -> 7; matrix products, arithmetic and copies ran while one was open for 1% -> 2% of each run, Pallas kernels for 0% -> 0%
where the time goes in v1:
time: 291 us; the launch traced here: 289 us
  waiting for transfers between devices  139 us (48%)
  blocking collectives  65.3 us (22%)
  starting transfers between devices  64.1 us (22%)
  local copies, waits for them, and re-layouts  9.95 us (3%)
  other arithmetic  6.42 us (2%)
  matrix products  2.96 us (1%)
    ppermute x7, waiting for transfers between devices, shifted(): return lax.ppermute(value, axis, pairs)  121 us
    all_to_all x1, blocking collectives, body(): lax.all_to_all(summed, 'tm', split_axis=0, concat_axis=2, tiled=True)  53.6 us
    ppermute x7, starting transfers between devices, shifted(): return lax.ppermute(value, axis, pairs)  45.2 us
    all_to_all x1, waiting for transfers between devices, body(): lax.all_to_all(rotor_coeffs.reshape(local_c, comp, rows, LANES), 'tm', sp...  14.2 us
    unnamed x1, blocking collectives  11.8 us
    all_to_all x1, starting transfers between devices, body(): lax.all_to_all(jnp.stack([stencil_offsets] * lax.axis_size('tm')), 'tm',...  8.69 us
    all_to_all x1, starting transfers between devices, body(): lax.all_to_all(rotor_coeffs.reshape(local_c, comp, rows, LANES), 'tm', sp...  6.65 us
  transfers between devices with their start and end apart: 10, of which 7 were waited for; matrix products, arithmetic and copies ran while one was open for 2% of the time, Pallas kernels for 0%

profile of v1, /device:TPU:97, one launch (start us, length us, event | category | flops | bytes accessed | tf_op | source)
XLA Modules:
  0.0 289.0 jit_solution(6917708720212373685)
XLA Ops:
  0.0 0.0 copy-start
  0.0 3.0 %copy.26 = f32[8,2,128,128]{3,1,0,2:T(2,128)} copy(f32[8,2,128,128]{3,2,1,0:T(8,128)} %bitcast.48) | data formatting | bytes 2097152 | tf_op jit(solution)/shard_map/reshape | solution.py:36
  3.0 6.7 %all-to-all-start.2 = ((f32[8,2,128,128]{3,1,0,2:T(2,128)}), f32[8,2,128,128]{3,1,0,2:T(2,128)S(1)}, u32[]{:S(2)}, u32[]{:S(2)}) async-start(f32[8,2,128,128]{3,1,0,2:T(2,128)} %copy.26), calls=%async_computation.2 | async-start | bytes 2097152 | tf_op jit(solution)/shard_map/all_to_all | solution.py:35
  9.7 14.2 %all-to-all-done.2 = f32[8,2,128,128]{3,1,0,2:T(2,128)S(1)} async-done(((f32[8,2,128,128]{3,1,0,2:T(2,128)}), f32[8,2,128,128]{3,1,0,2:T(2,128)S(1)}, u32[]{:S(2)}, u32[]{:S(2)}) %all-to-all-start.2) | async-done | bytes 1048608 | tf_op jit(solution)/shard_map/all_to_all | solution.py:35
  23.9 0.3 copy.27
  24.2 1.8 fusion
  26.0 2.9 %collective-permute-start = (f32[64,2,16,128]{3,0,2,1:T(8,128)S(1)}, f32[64,2,16,128]{3,0,2,1:T(8,128)S(1)}, u32[]{:S(2)}, u32[]{:S(2)}) collective-permute-start(f32[64,2,16,128]{3,0,2,1:T(8,128)S(1)} %fusion), channel_id=1, source_target_pairs={{0,1},{1,2},{2,3},{3,4},{4,5},{5,6},{6,7},{7,8},{8,9},{9,10},{10,1... | collective-permute-start | bytes 3145736 | tf_op jit(solution)/shard_map/ppermute | solution.py:14
  28.9 0.0 copy-start.5
  28.9 0.7 copy-done.5
  29.6 0.6 dynamic-slice
  30.8 0.0 copy-start.4
  30.8 0.6 copy-done.4
  31.4 0.2 dynamic-update-slice
  31.6 11.8 %all-reduce = s32[64]{0:T(128)S(1)} all-reduce(s32[64]{0:T(128)S(1)} %dynamic-update-slice), channel_id=1, replica_groups=mesh['tm'=8,'azim'=32] {'tm'}, use_global_device_ids=true, to_apply=%add | all-reduce | flops 64 | bytes 512
  43.4 0.0 collective-permute-done
  43.4 0.2 broadcast_select_fusion
  43.7 1.0 collective-permute-start.1
  44.7 24.2 %collective-permute-done.1 = f32[64,2,16,128]{3,0,2,1:T(8,128)S(1)} collective-permute-done((f32[64,2,16,128]{3,0,2,1:T(8,128)S(1)}, f32[64,2,16,128]{3,0,2,1:T(8,128)S(1)}, u32[]{:S(2)}, u32[]{:S(2)}) %collective-permute-start.1) | collective-permute-done | bytes 1048608 | tf_op jit(solution)/shard_map/ppermute | solution.py:14
  68.9 0.2 broadcast_select_fusion.1
  69.2 3.4 %collective-permute-start.2 = (f32[64,2,16,128]{3,0,2,1:T(8,128)S(1)}, f32[64,2,16,128]{3,0,2,1:T(8,128)S(1)}, u32[]{:S(2)}, u32[]{:S(2)}) collective-permute-start(f32[64,2,16,128]{3,0,2,1:T(8,128)S(1)} %broadcast_select_fusion.1), channel_id=1, source_target_pairs={{0,4},{1,5},{2,6},{3,7},{4,8},{5,9},{6,10},{7,11},{8,12},{9,13},{1... | collective-permute-start | bytes 3145736 | tf_op jit(solution)/shard_map/ppermute | solution.py:14
  72.6 20.1 %collective-permute-done.2 = f32[64,2,16,128]{3,0,2,1:T(8,128)S(1)} collective-permute-done((f32[64,2,16,128]{3,0,2,1:T(8,128)S(1)}, f32[64,2,16,128]{3,0,2,1:T(8,128)S(1)}, u32[]{:S(2)}, u32[]{:S(2)}) %collective-permute-start.2) | collective-permute-done | bytes 1048608 | tf_op jit(solution)/shard_map/ppermute | solution.py:14
  92.7 0.2 broadcast_select_fusion.2
  93.0 2.8 collective-permute-start.3
  95.7 28.5 %collective-permute-done.3 = f32[64,2,16,128]{3,0,2,1:T(8,128)S(1)} collective-permute-done((f32[64,2,16,128]{3,0,2,1:T(8,128)S(1)}, f32[64,2,16,128]{3,0,2,1:T(8,128)S(1)}, u32[]{:S(2)}, u32[]{:S(2)}) %collective-permute-start.3) | collective-permute-done | bytes 1048608 | tf_op jit(solution)/shard_map/ppermute | solution.py:14
  124.2 0.0 copy-start.3
  124.2 0.0 copy-start.2
  124.2 0.2 broadcast_select_fusion.3
  124.5 5.7 %collective-permute-start.4 = (f32[64,2,16,128]{3,0,2,1:T(8,128)S(1)}, f32[64,2,16,128]{3,0,2,1:T(8,128)}, u32[]{:S(2)}, u32[]{:S(2)}) collective-permute-start(f32[64,2,16,128]{3,0,2,1:T(8,128)S(1)} %broadcast_select_fusion.3), channel_id=1, source_target_pairs={{0,16},{1,17},{2,18},{3,19},{4,20},{5,21},{6,22},{7,23},{8,24},{9,... | collective-permute-start | bytes 3145736 | tf_op jit(solution)/shard_map/ppermute | solution.py:14
  130.2 0.0 copy-done.3
  130.2 0.6 stack.2
  130.8 8.7 %all-to-all-start.1 = ((s32[8,8,2]{1,2,0:T(2,128)}), s32[8,8,2]{1,2,0:T(2,128)S(1)}, u32[]{:S(2)}, u32[]{:S(2)}) async-start(s32[8,8,2]{1,2,0:T(2,128)} %stack.2), calls=%async_computation.1 | async-start | bytes 16384 | tf_op jit(solution)/shard_map/all_to_all | solution.py:51
  139.5 0.0 copy-done.2
  139.5 1.8 copy.22
  141.2 4.8 %all-to-all-done.1 = s32[8,8,2]{1,2,0:T(2,128)S(1)} async-done(((s32[8,8,2]{1,2,0:T(2,128)}), s32[8,8,2]{1,2,0:T(2,128)S(1)}, u32[]{:S(2)}, u32[]{:S(2)}) %all-to-all-start.1) | async-done | bytes 544 | tf_op jit(solution)/shard_map/all_to_all | solution.py:51
  146.0 3.6 %all-to-all-start = ((f32[8,2,128,128]{3,1,0,2:T(2,128)}), f32[8,2,128,128]{3,1,0,2:T(2,128)S(1)}, u32[]{:S(2)}, u32[]{:S(2)}) async-start(f32[8,2,128,128]{3,1,0,2:T(2,128)} %copy.22), calls=%async_computation | async-start | bytes 2097152 | tf_op jit(solution)/shard_map/all_to_all | solution.py:42
  149.6 24.9 %collective-permute-done.4 = f32[64,2,16,128]{3,0,2,1:T(8,128)} collective-permute-done((f32[64,2,16,128]{3,0,2,1:T(8,128)S(1)}, f32[64,2,16,128]{3,0,2,1:T(8,128)}, u32[]{:S(2)}, u32[]{:S(2)}) %collective-permute-start.4) | collective-permute-done | bytes 1048608 | tf_op jit(solution)/shard_map/ppermute | solution.py:14
  174.5 1.4 broadcast_select_fusion.4
  175.9 29.4 %collective-permute-start.6 = (f32[64,2,16,128]{3,0,2,1:T(8,128)S(1)}, f32[64,2,16,128]{3,0,2,1:T(8,128)S(1)}, u32[]{:S(2)}, u32[]{:S(2)}) collective-permute-start(f32[64,2,16,128]{3,0,2,1:T(8,128)S(1)} %broadcast_select_fusion.4), channel_id=1, source_target_pairs={{0,1},{1,2},{2,3},{3,4},{4,5},{5,6},{6,7},{7,8},{8,9},{9,10},{10,1... | collective-permute-start | bytes 3145736 | tf_op jit(solution)/shard_map/ppermute | solution.py:14
  205.3 0.0 collective-permute-start.5
  205.3 0.0 copy-done
  205.4 0.1 reshape.114
  205.4 0.0 all-to-all-done
  205.5 0.1 copy.44
  205.6 0.1 slice_bitcast_fusion.1
  205.7 22.7 %collective-permute-done.6 = f32[64,2,16,128]{3,0,2,1:T(8,128)S(1)} collective-permute-done((f32[64,2,16,128]{3,0,2,1:T(8,128)S(1)}, f32[64,2,16,128]{3,0,2,1:T(8,128)S(1)}, u32[]{:S(2)}, u32[]{:S(2)}) %collective-permute-start.6) | collective-permute-done | bytes 1048608 | tf_op jit(solution)/shard_map/ppermute | solution.py:14
  228.3 0.0 collective-permute-done.5
  228.3 1.9 multiply_reduce_fusion
  230.2 0.1 fusion.6
  230.3 1.2 fusion.3
  231.5 0.6 copy.30
  232.1 53.6 %all_to_all.56 = f32[64,2,16,128]{3,2,1,0:T(8,128)S(1)} all-to-all(f32[64,2,16,128]{3,2,1,0:T(8,128)S(1)} %copy.30), channel_id=1, replica_groups=mesh['tm'=8,'azim'=32] {'tm'}, dimensions={0} | all-to-all | bytes 2097152 | tf_op jit(solution)/shard_map/all_to_all | solution.py:79
  285.7 0.0 copy-start.1
  285.7 0.1 copy.31
  285.8 1.1 copy-done.1
  286.9 2.1 sub.12
  (7 shorter events, 0.0 us)
Async XLA Ops:
  0.0 205.3 %copy-start = (f32[1,16384]{1,0:T(1,128)S(1)}, f32[1,16384]{1,0:T(1,128)}, u32[]{:S(2)}) copy-start(f32[1,16384]{1,0:T(1,128)} %param.10) | copy-start | bytes 196612
  3.0 20.8 %all-to-all-start.2 = ((f32[8,2,128,128]{3,1,0,2:T(2,128)}), f32[8,2,128,128]{3,1,0,2:T(2,128)S(1)}, u32[]{:S(2)}, u32[]{:S(2)}) async-start(f32[8,2,128,128]{3,1,0,2:T(2,128)} %copy.26), calls=%async_computation.2 | async-start | bytes 2097152 | tf_op jit(solution)/shard_map/all_to_all | solution.py:35
  26.0 17.4 %collective-permute-start = (f32[64,2,16,128]{3,0,2,1:T(8,128)S(1)}, f32[64,2,16,128]{3,0,2,1:T(8,128)S(1)}, u32[]{:S(2)}, u32[]{:S(2)}) collective-permute-start(f32[64,2,16,128]{3,0,2,1:T(8,128)S(1)} %fusion), channel_id=1, source_target_pairs={{0,1},{1,2},{2,3},{3,4},{4,5},{5,6},{6,7},{7,8},{8,9},{9,10},{10,1... | collective-permute-start | bytes 3145736 | tf_op jit(solution)/shard_map/ppermute | solution.py:14
  28.9 0.7 copy-start.5
  30.8 0.7 copy-start.4
  43.7 25.3 %collective-permute-start.1 = (f32[64,2,16,128]{3,0,2,1:T(8,128)S(1)}, f32[64,2,16,128]{3,0,2,1:T(8,128)S(1)}, u32[]{:S(2)}, u32[]{:S(2)}) collective-permute-start(f32[64,2,16,128]{3,0,2,1:T(8,128)S(1)} %broadcast_select_fusion), channel_id=1, source_target_pairs={{0,2},{1,3},{2,4},{3,5},{4,6},{5,7},{6,8},{7,9},{8,10},{9,11},{10,... | collective-permute-start | bytes 3145736 | tf_op jit(solution)/shard_map/ppermute | solution.py:14
  69.2 23.6 %collective-permute-start.2 = (f32[64,2,16,128]{3,0,2,1:T(8,128)S(1)}, f32[64,2,16,128]{3,0,2,1:T(8,128)S(1)}, u32[]{:S(2)}, u32[]{:S(2)}) collective-permute-start(f32[64,2,16,128]{3,0,2,1:T(8,128)S(1)} %broadcast_select_fusion.1), channel_id=1, source_target_pairs={{0,4},{1,5},{2,6},{3,7},{4,8},{5,9},{6,10},{7,11},{8,12},{9,13},{1... | collective-permute-start | bytes 3145736 | tf_op jit(solution)/shard_map/ppermute | solution.py:14
  93.0 31.3 %collective-permute-start.3 = (f32[64,2,16,128]{3,0,2,1:T(8,128)S(1)}, f32[64,2,16,128]{3,0,2,1:T(8,128)S(1)}, u32[]{:S(2)}, u32[]{:S(2)}) collective-permute-start(f32[64,2,16,128]{3,0,2,1:T(8,128)S(1)} %broadcast_select_fusion.2), channel_id=1, source_target_pairs={{0,8},{1,9},{2,10},{3,11},{4,12},{5,13},{6,14},{7,15},{8,16},{9,17... | collective-permute-start | bytes 3145736 | tf_op jit(solution)/shard_map/ppermute | solution.py:14
  124.2 5.9 %copy-start.3 = (s32[8,2]{0,1:T(2,128)S(1)}, s32[8,2]{0,1:T(2,128)}, u32[]{:S(2)}) copy-start(s32[8,2]{0,1:T(2,128)} %param.9) | copy-start | bytes 196
  124.2 15.2 %copy-start.2 = (f32[8,2,1,16384]{3,2,1,0:T(1,128)S(1)}, f32[8,2,1,16384]{3,2,1,0:T(1,128)}, u32[]{:S(2)}) copy-start(f32[8,2,1,16384]{3,2,1,0:T(1,128)} %param.7) | copy-start | bytes 3145732
  124.5 50.0 %collective-permute-start.4 = (f32[64,2,16,128]{3,0,2,1:T(8,128)S(1)}, f32[64,2,16,128]{3,0,2,1:T(8,128)}, u32[]{:S(2)}, u32[]{:S(2)}) collective-permute-start(f32[64,2,16,128]{3,0,2,1:T(8,128)S(1)} %broadcast_select_fusion.3), channel_id=1, source_target_pairs={{0,16},{1,17},{2,18},{3,19},{4,20},{5,21},{6,22},{7,23},{8,24},{9,... | collective-permute-start | bytes 3145736 | tf_op jit(solution)/shard_map/ppermute | solution.py:14
  130.8 15.2 %all-to-all-start.1 = ((s32[8,8,2]{1,2,0:T(2,128)}), s32[8,8,2]{1,2,0:T(2,128)S(1)}, u32[]{:S(2)}, u32[]{:S(2)}) async-start(s32[8,8,2]{1,2,0:T(2,128)} %stack.2), calls=%async_computation.1 | async-start | bytes 16384 | tf_op jit(solution)/shard_map/all_to_all | solution.py:51
  146.0 59.5 %all-to-all-start = ((f32[8,2,128,128]{3,1,0,2:T(2,128)}), f32[8,2,128,128]{3,1,0,2:T(2,128)S(1)}, u32[]{:S(2)}, u32[]{:S(2)}) async-start(f32[8,2,128,128]{3,1,0,2:T(2,128)} %copy.22), calls=%async_computation | async-start | bytes 2097152 | tf_op jit(solution)/shard_map/all_to_all | solution.py:42
  175.9 52.4 %collective-permute-start.6 = (f32[64,2,16,128]{3,0,2,1:T(8,128)S(1)}, f32[64,2,16,128]{3,0,2,1:T(8,128)S(1)}, u32[]{:S(2)}, u32[]{:S(2)}) collective-permute-start(f32[64,2,16,128]{3,0,2,1:T(8,128)S(1)} %broadcast_select_fusion.4), channel_id=1, source_target_pairs={{0,1},{1,2},{2,3},{3,4},{4,5},{5,6},{6,7},{7,8},{8,9},{9,10},{10,1... | collective-permute-start | bytes 3145736 | tf_op jit(solution)/shard_map/ppermute | solution.py:14
  205.3 23.0 %collective-permute-start.5 = (f32[64,2,16,128]{3,0,2,1:T(8,128)S(1)}, f32[64,2,16,128]{3,0,2,1:T(8,128)}, u32[]{:S(2)}, u32[]{:S(2)}) collective-permute-start(f32[64,2,16,128]{3,0,2,1:T(8,128)S(1)} %broadcast_select_fusion.4), channel_id=1, source_target_pairs={{0,31},{1,0},{2,1},{3,2},{4,3},{5,4},{6,5},{7,6},{8,7},{9,8},{10,9... | collective-permute-start | bytes 3145736 | tf_op jit(solution)/shard_map/ppermute | solution.py:14
  285.7 1.2 copy-start.1
